TPU v7x, 256 devices: a whole 4x4x8 slice. The times are simulated.
256 devices in a mesh: samp: 32 (over z_hi, y, x), feat: 8 (over z_lo, core).
Axes of the slice: x: 4, y: 4, z: 8 (z_hi: 2, z_lo: 4; z = z_hi * 4 + z_lo), core: 2. Of those that a mesh axis runs over, the one named last changes fastest.
Arguments:
- counters: bfloat16 [32768, 512], P('samp'), may hold values from -6 to 6
- frequencies: bfloat16 [512, 4096], P(None, 'feat'), may hold values from -0.25 to 0.25
- phases: bfloat16 [1, 4096], P(None, 'feat'), may hold values from -3.140625 to 3.140625
- targets: bfloat16 [32768, 64], P('samp'), may hold values from -6 to 6
Outputs:
- solution: float32 [4096, 64], P('samp')
- residual: float32 [4096, 64], P('samp')
- gram: float32 [4096, 4096], P('samp', 'feat')
All inputs are finite; a program needn't handle non-finite values.
Results may differ from a plain program's by a relative error of at most 0.0035.
Values may be sent and summed in bfloat16 or wider, within the bound.
A program may use at most 64 MiB of HBM per device.

v0:
```python
import math
import jax
import jax.numpy as jnp
from jax import lax
from jax.sharding import PartitionSpec as P

ITERS = 2
RIDGE = 0.05


def on_device(counters, frequencies, phases, targets):
    rows = counters.shape[0]
    block_width = frequencies.shape[1]
    mixed = jnp.dot(counters, frequencies, preferred_element_type=jnp.float32)
    local_feats = jnp.cos(mixed + phases.astype(jnp.float32)).astype(jnp.bfloat16)
    features_all = lax.all_gather(local_feats, "feat", axis=1, tiled=True)
    joined = jnp.concatenate([local_feats, targets], axis=1)
    inner = (((0,), (0,)), ((), ()))
    reduced = lax.psum_scatter(
        lax.dot_general(features_all, joined, inner, preferred_element_type=jnp.float32),
        "samp",
        scatter_dimension=0,
        tiled=True,
    )
    samples = rows * lax.axis_size("samp")
    gram_block = reduced[:, :block_width] / samples
    right_side = reduced[:, block_width:] / math.sqrt(samples)
    feat_offset = lax.axis_index("feat") * block_width

    def squares(vector):
        return lax.psum(jnp.sum(vector * vector, axis=0), "samp")

    solution = jnp.zeros_like(right_side)
    residual = right_side
    direction = right_side
    norm_now = squares(residual)
    for iteration in range(ITERS):
        gathered = lax.all_gather(direction, "samp", axis=0, tiled=True)
        selected = lax.dynamic_slice_in_dim(gathered, feat_offset, block_width, 0)
        partial_value = jnp.dot(gram_block, selected, precision=lax.Precision.HIGHEST)
        image = lax.psum(partial_value, "feat") + RIDGE * direction
        curve = lax.psum(jnp.sum(direction * image, axis=0), "samp")
        step_size = norm_now / curve
        solution = solution + step_size * direction
        residual = residual - step_size * image
        norm_next = squares(residual)
        direction = residual + norm_next / norm_now * direction
        norm_now = norm_next
    return (solution, residual, gram_block)


def solution(mesh):
    return jax.shard_map(
        on_device,
        mesh=mesh,
        in_specs=(P("samp", None), P(None, "feat"), P(None, "feat"), P("samp", None)),
        out_specs=(P("samp", None), P("samp", None), P("samp", "feat")),
        check_vma=False,
    )
```

profile of v0, /device:TPU:128, one launch (start us, length us, event | category | flops | bytes accessed | tf_op | source)
XLA Modules:
  0.0 973.0 jit_solution(9429398603258121843)
XLA Ops:
  7.2 0.0 copy-start
  7.2 0.0 all-gather.4.cloned.1.call-start
  7.2 0.8 add.52
  8.0 0.4 copy-done
  8.4 0.0 copy-start.1
  8.4 9.2 cosine_convert_fusion
  17.6 0.0 all-gather.4.cloned.1.call-update
  17.6 0.0 reduce-scatter.2.cloned.1.call-start
  17.7 93.0 %all-gather.4.cloned.1.call-done = bf16[1024,4096]{0,1:T(8,128)(2,1)} async-done(((bf16[1024,512]{0,1:T(8,128)(2,1)}), bf16[1024,4096]{0,1:T(8,128)(2,1)}) %all-gather.4.cloned.1.call-update) | async-done | bytes 8388624 | tf_op jit(solution)/shard_map/all_gather | solution.py:16
  110.7 0.0 copy-done.1
  110.7 9.9 %fusion = f32[4096,576]{0,1:T(8,128)} fusion(bf16[1024,4096]{0,1:T(8,128)(2,1)} %all-gather.4.cloned.1.call-done, bf16[1024,64]{0,1:T(8,128)(2,1)S(1)} %copy-done.1, bf16[1024,512]{0,1:T(8,128)(2,1)} %cosine_convert_fusion), kind=kOutput, calls=%fused_computation.1 | convolution fusion | flops 4834197504 | bytes 19005440 | tf_op jit(solution)/shard_map/dot_general | solution.py:20
  120.6 0.0 reduce-scatter.2.cloned.1.call-update
  120.6 0.0 all-gather.6.cloned.1.call-start
  120.7 283.7 %reduce-scatter.2.cloned.1.call-done = f32[128,576]{0,1:T(8,128)} async-done(((f32[4096,576]{0,1:T(8,128)}), f32[128,576]{0,1:T(8,128)}) %reduce-scatter.2.cloned.1.call-update) | async-done | bytes 294928 | tf_op jit(solution)/shard_map/reduce_scatter | solution.py:19
  404.4 1.4 slice_multiply_fusion.1
  405.7 0.0 all-gather.6.cloned.1.call-update
  405.8 0.0 all-gather.8.cloned.1.call-start
  405.8 79.4 %all-gather.6.cloned.1.call-done = f32[4096,64]{0,1:T(8,128)} async-done(((f32[128,64]{0,1:T(8,128)}), f32[4096,64]{0,1:T(8,128)}) %all-gather.6.cloned.1.call-update) | async-done | bytes 1048592 | tf_op jit(solution)/shard_map/all_gather | solution.py:38
  485.2 1.3 fusion.6
  486.5 29.9 %psum.43 = f32[128,64]{0,1:T(8,128)S(1)} all-reduce(f32[128,64]{0,1:T(8,128)S(1)} %fusion.6), channel_id=1, replica_groups=mesh['samp'=32,'feat'=8] {'feat'}, use_global_device_ids=true, to_apply=%region_3.0 | all-reduce | flops 8192 | bytes 65536 | tf_op jit(solution)/shard_map/psum | solution.py:41
  516.4 0.9 multiply_reduce_fusion.2
  517.3 115.8 %all-reduce = (f32[64]{0:T(128)S(1)}, f32[64]{0:T(128)S(1)}) all-reduce(f32[64]{0:T(128)S(1)} %get-tuple-element.7, f32[64]{0:T(128)S(1)} %get-tuple-element.6), channel_id=1, replica_groups=mesh['samp'=32,'feat'=8] {'samp'}, use_global_device_ids=true, to_apply=%region_2.0 | all-reduce | flops 128 | bytes 1024 | tf_op jit(solution)/shard_map/psum | solution.py:31
  633.1 0.9 multiply_reduce_fusion.1
  634.0 108.1 %psum.45 = f32[64]{0:T(128)S(1)} all-reduce(f32[64]{0:T(128)S(1)} %get-tuple-element.12), channel_id=1, replica_groups=mesh['samp'=32,'feat'=8] {'samp'}, use_global_device_ids=true, to_apply=%region_7.0 | all-reduce | flops 64 | bytes 512 | tf_op jit(solution)/shard_map/psum | solution.py:31
  742.1 1.5 multiply_add_fusion.2
  743.6 0.0 all-gather.8.cloned.1.call-update
  743.6 1.0 slice_multiply_fusion
  744.6 0.8 copy.7
  745.4 71.7 %all-gather.8.cloned.1.call-done = f32[4096,64]{0,1:T(8,128)} async-done(((f32[128,64]{0,1:T(8,128)}), f32[4096,64]{0,1:T(8,128)}) %all-gather.8.cloned.1.call-update) | async-done | bytes 1048592 | tf_op jit(solution)/shard_map/all_gather | solution.py:38
  817.1 1.3 fusion.4
  818.4 29.9 %psum.46 = f32[128,64]{0,1:T(8,128)S(1)} all-reduce(f32[128,64]{0,1:T(8,128)S(1)} %fusion.4), channel_id=1, replica_groups=mesh['samp'=32,'feat'=8] {'feat'}, use_global_device_ids=true, to_apply=%region_8.0 | all-reduce | flops 8192 | bytes 65536 | tf_op jit(solution)/shard_map/psum | solution.py:41
  848.3 0.9 multiply_reduce_fusion
  849.2 115.8 %psum.47 = f32[64]{0:T(128)S(1)} all-reduce(f32[64]{0:T(128)S(1)} %multiply_reduce_fusion), channel_id=1, replica_groups=mesh['samp'=32,'feat'=8] {'samp'}, use_global_device_ids=true, to_apply=%region_10.0 | all-reduce | flops 64 | bytes 512 | tf_op jit(solution)/shard_map/psum | solution.py:42
  965.0 1.5 multiply_subtract_fusion
  (3 shorter events, 0.0 us)
Async XLA Ops:
  7.2 1.2 copy-start
  7.2 103.5 %all-gather.4.cloned.1.call-start = ((), (), s32[]{:S(2)}) async-start(), calls=%async_computation.1 | async-start | bytes 9437184 | tf_op jit(solution)/shard_map/all_gather | solution.py:16
  8.4 102.2 %copy-start.1 = (bf16[1024,64]{0,1:T(8,128)(2,1)S(1)}, bf16[1024,64]{0,1:T(8,128)(2,1)}, u32[]{:S(2)}) copy-start(bf16[1024,64]{0,1:T(8,128)(2,1)} %param.7) | copy-start | bytes 393220
  17.6 386.7 %reduce-scatter.2.cloned.1.call-start = ((), (), s32[]{:S(2)}) async-start(), calls=%async_computation.2 | async-start | bytes 9732096 | tf_op jit(solution)/shard_map/reduce_scatter | solution.py:19
  120.6 364.6 %all-gather.6.cloned.1.call-start = ((), (), s32[]{:S(2)}) async-start(), calls=%async_computation.3 | async-start | bytes 1081344 | tf_op jit(solution)/shard_map/all_gather | solution.py:38
  405.8 411.4 %all-gather.8.cloned.1.call-start = ((), (), s32[]{:S(2)}) async-start(), calls=%async_computation.4 | async-start | bytes 1081344 | tf_op jit(solution)/shard_map/all_gather | solution.py:38
Sparse Core Ops, SparseCore 0:
  17.8 92.8 all-gather.3
  120.7 283.5 reduce-scatter.1
  408.7 76.5 all-gather.5
  743.7 73.3 all-gather.7
where the time goes:
time: 974 us; the launch traced here: 973 us
  waiting for transfers between devices  528 us (54%)
  blocking collectives  399 us (41%)
  matrix products  21.7 us (2%)
  between operations  13.8 us (1%)
    reduce_scatter x1, waiting for transfers between devices, on_device(): lax.psum_scatter(lax.dot_general(features_all, joined, inner, preferred_e...  284 us
    psum x2, blocking collectives, squares(): return lax.psum(jnp.sum(vector * vector, axis=0), 'samp')  224 us
    all_gather x2, waiting for transfers between devices, on_device(): gathered = lax.all_gather(direction, 'samp', axis=0, tiled=True)  151 us
    psum x1, blocking collectives, on_device(): curve = lax.psum(jnp.sum(direction * image, axis=0), 'samp')  116 us
    all_gather x1, waiting for transfers between devices, on_device(): features_all = lax.all_gather(local_feats, 'feat', axis=1, tiled=True)  93 us
    psum x2, blocking collectives, on_device(): image = lax.psum(partial_value, 'feat') + RIDGE * direction  59.8 us
  transfers between devices with their start and end apart: 4, of which 4 were waited for; matrix products, arithmetic and copies ran while one was open for 0% of the time, Pallas kernels for 0%

commit v1 on v0

--- a/solution.py
+++ b/solution.py
@@ -35,7 +35,9 @@
     direction = right_side
     norm_now = squares(residual)
     for iteration in range(ITERS):
-        gathered = lax.all_gather(direction, "samp", axis=0, tiled=True)
+        gathered = jnp.concatenate(
+            lax.all_to_all(jnp.stack([direction] * lax.axis_size("samp")), "samp", 0, 0), axis=0
+        )
         selected = lax.dynamic_slice_in_dim(gathered, feat_offset, block_width, 0)
         partial_value = jnp.dot(gram_block, selected, precision=lax.Precision.HIGHEST)
         image = lax.psum(partial_value, "feat") + RIDGE * direction

time: 974 us -> 868 us (0.89)
  waiting for transfers between devices: 528 us -> 406 us
  starting transfers between devices: 0.16 us -> 18.7 us
    all_gather x2 -> x0, waiting for transfers between devices: 151 us -> none  [on_device(): gathered = lax.all_gather(direction, 'samp', axis=0, tiled=True)]
    all_to_all x0 -> x2, waiting for transfers between devices: none -> 29.6 us  [on_device(): lax.all_to_all(jnp.stack([direction] * lax.axis_size('samp')), 'samp', 0, 0)]
    all_to_all x0 -> x2, starting transfers between devices: none -> 18.6 us  [on_device(): lax.all_to_all(jnp.stack([direction] * lax.axis_size('samp')), 'samp', 0, 0)]
where the time goes in v1:
time: 868 us; the launch traced here: 863 us
  waiting for transfers between devices  406 us (47%)
  blocking collectives  398 us (46%)
  matrix products  19.8 us (2%)
  starting transfers between devices  18.7 us (2%)
  between operations  14.1 us (2%)
    reduce_scatter x1, waiting for transfers between devices, on_device(): lax.psum_scatter(lax.dot_general(features_all, joined, inner, preferred_e...  284 us
    psum x2, blocking collectives, squares(): return lax.psum(jnp.sum(vector * vector, axis=0), 'samp')  226 us
    psum x1, blocking collectives, on_device(): curve = lax.psum(jnp.sum(direction * image, axis=0), 'samp')  111 us
    all_gather x1, waiting for transfers between devices, on_device(): features_all = lax.all_gather(local_feats, 'feat', axis=1, tiled=True)  93 us
    psum x2, blocking collectives, on_device(): image = lax.psum(partial_value, 'feat') + RIDGE * direction  60.8 us
    all_to_all x2, waiting for transfers between devices, on_device(): lax.all_to_all(jnp.stack([direction] * lax.axis_size('samp')), 'samp', 0, 0)  29.6 us
    all_to_all x2, starting transfers between devices, on_device(): lax.all_to_all(jnp.stack([direction] * lax.axis_size('samp')), 'samp', 0, 0)  18.6 us
  transfers between devices with their start and end apart: 4, of which 4 were waited for; matrix products, arithmetic and copies ran while one was open for 0% of the time, Pallas kernels for 0%

profile of v1, /device:TPU:128, one launch (start us, length us, event | category | flops | bytes accessed | tf_op | source)
XLA Modules:
  0.0 862.9 jit_solution(8468425917946293748)
XLA Ops:
  7.2 0.0 copy-start
  7.2 0.0 all-gather.2.cloned.1.call-start
  7.2 0.8 add.52
  8.0 0.4 copy-done
  8.4 0.0 copy-start.2
  8.4 9.2 %cosine_convert_fusion = bf16[1024,512]{0,1:T(8,128)(2,1)} fusion(bf16[1024,512]{1,0:T(8,128)(2,1)S(1)} %copy-done, bf16[512,512]{1,0:T(8,128)(2,1)} %param.5, f32[512]{0:T(512)S(1)} %bitcast.14), kind=kOutput, calls=%fused_computation | convolution fusion | flops 537919488 | bytes 2623488 | tf_op jit(solution)/shard_map/dot_general | solution.py:14
  17.6 0.0 all-gather.2.cloned.1.call-update
  17.6 0.0 reduce-scatter.2.cloned.1.call-start
  17.7 93.0 %all-gather.2.cloned.1.call-done = bf16[1024,4096]{0,1:T(8,128)(2,1)} async-done(((bf16[1024,512]{0,1:T(8,128)(2,1)}), bf16[1024,4096]{0,1:T(8,128)(2,1)}) %all-gather.2.cloned.1.call-update) | async-done | bytes 8388624 | tf_op jit(solution)/shard_map/all_gather | solution.py:16
  110.7 0.0 copy-done.2
  110.7 9.9 %fusion = f32[4096,576]{0,1:T(8,128)} fusion(bf16[1024,4096]{0,1:T(8,128)(2,1)} %all-gather.2.cloned.1.call-done, bf16[1024,64]{0,1:T(8,128)(2,1)S(1)} %copy-done.2, bf16[1024,512]{0,1:T(8,128)(2,1)} %cosine_convert_fusion), kind=kOutput, calls=%fused_computation.1 | convolution fusion | flops 4834197504 | bytes 19005440 | tf_op jit(solution)/shard_map/dot_general | solution.py:20
  120.6 0.0 reduce-scatter.2.cloned.1.call-update
  120.6 283.7 %reduce-scatter.2.cloned.1.call-done = f32[128,576]{0,1:T(8,128)} async-done(((f32[4096,576]{0,1:T(8,128)}), f32[128,576]{0,1:T(8,128)}) %reduce-scatter.2.cloned.1.call-update) | async-done | bytes 294928 | tf_op jit(solution)/shard_map/reduce_scatter | solution.py:19
  404.4 0.8 slice_multiply_fusion.1
  405.1 1.1 stack.4
  406.2 0.0 copy-start.1
  406.2 11.2 %all-to-all-start = ((f32[32,128,64]{1,2,0:T(8,128)}), f32[32,128,64]{1,2,0:T(8,128)S(1)}, u32[]{:S(2)}, u32[]{:S(2)}) async-start(f32[32,128,64]{1,2,0:T(8,128)} %stack.4), calls=%async_computation.1 | async-start | bytes 2097152 | tf_op jit(solution)/shard_map/all_to_all | solution.py:39
  417.5 14.5 %all-to-all-done = f32[32,128,64]{1,2,0:T(8,128)S(1)} async-done(((f32[32,128,64]{1,2,0:T(8,128)}), f32[32,128,64]{1,2,0:T(8,128)S(1)}, u32[]{:S(2)}, u32[]{:S(2)}) %all-to-all-start) | async-done | bytes 1048608 | tf_op jit(solution)/shard_map/all_to_all | solution.py:39
  432.0 0.1 copy_bitcast_fusion.1
  432.1 0.0 copy-done.1
  432.1 0.3 fusion.6
  432.4 34.9 %psum.43 = f32[128,64]{0,1:T(8,128)S(1)} all-reduce(f32[128,64]{0,1:T(8,128)S(1)} %fusion.6), channel_id=1, replica_groups=mesh['samp'=32,'feat'=8] {'feat'}, use_global_device_ids=true, to_apply=%region_3.0 | all-reduce | flops 8192 | bytes 65536 | tf_op jit(solution)/shard_map/psum | solution.py:43
  467.2 0.1 multiply_reduce_fusion.2
  467.4 115.6 %all-reduce = (f32[64]{0:T(128)S(1)}, f32[64]{0:T(128)S(1)}) all-reduce(f32[64]{0:T(128)S(1)} %get-tuple-element.13, f32[64]{0:T(128)S(1)} %get-tuple-element.12), channel_id=1, replica_groups=mesh['samp'=32,'feat'=8] {'samp'}, use_global_device_ids=true, to_apply=%region_2.0 | all-reduce | flops 128 | bytes 1024 | tf_op jit(solution)/shard_map/psum | solution.py:31
  583.0 0.2 multiply_reduce_fusion.1
  583.2 110.5 %psum.45 = f32[64]{0:T(128)S(1)} all-reduce(f32[64]{0:T(128)S(1)} %get-tuple-element.18), channel_id=1, replica_groups=mesh['samp'=32,'feat'=8] {'samp'}, use_global_device_ids=true, to_apply=%region_7.0 | all-reduce | flops 64 | bytes 512 | tf_op jit(solution)/shard_map/psum | solution.py:31
  693.7 0.1 multiply_add_fusion.2
  693.8 1.1 stack.5
  694.9 7.4 all-to-all-start.1
  702.3 0.8 copy.13
  703.2 15.1 %all-to-all-done.1 = f32[32,128,64]{1,2,0:T(8,128)S(1)} async-done(((f32[32,128,64]{1,2,0:T(8,128)}), f32[32,128,64]{1,2,0:T(8,128)S(1)}, u32[]{:S(2)}, u32[]{:S(2)}) %all-to-all-start.1) | async-done | bytes 1048608 | tf_op jit(solution)/shard_map/all_to_all | solution.py:39
  718.2 0.1 copy_bitcast_fusion
  718.3 0.3 fusion.4
  718.6 25.9 %psum.46 = f32[128,64]{0,1:T(8,128)S(1)} all-reduce(f32[128,64]{0,1:T(8,128)S(1)} %fusion.4), channel_id=1, replica_groups=mesh['samp'=32,'feat'=8] {'feat'}, use_global_device_ids=true, to_apply=%region_8.0 | all-reduce | flops 8192 | bytes 65536 | tf_op jit(solution)/shard_map/psum | solution.py:43
  744.6 0.1 multiply_reduce_fusion
  744.7 110.7 %psum.47 = f32[64]{0:T(128)S(1)} all-reduce(f32[64]{0:T(128)S(1)} %multiply_reduce_fusion), channel_id=1, replica_groups=mesh['samp'=32,'feat'=8] {'samp'}, use_global_device_ids=true, to_apply=%region_10.0 | all-reduce | flops 64 | bytes 512 | tf_op jit(solution)/shard_map/psum | solution.py:44
  855.3 0.7 multiply_subtract_fusion
  (4 shorter events, 0.0 us)
Async XLA Ops:
  7.2 1.2 copy-start
  7.2 103.5 %all-gather.2.cloned.1.call-start = ((), (), s32[]{:S(2)}) async-start(), calls=%async_computation.3 | async-start | bytes 9437184 | tf_op jit(solution)/shard_map/all_gather | solution.py:16
  8.4 102.2 %copy-start.2 = (bf16[1024,64]{0,1:T(8,128)(2,1)S(1)}, bf16[1024,64]{0,1:T(8,128)(2,1)}, u32[]{:S(2)}) copy-start(bf16[1024,64]{0,1:T(8,128)(2,1)} %param.7) | copy-start | bytes 393220
  17.6 386.7 %reduce-scatter.2.cloned.1.call-start = ((), (), s32[]{:S(2)}) async-start(), calls=%async_computation.4 | async-start | bytes 9732096 | tf_op jit(solution)/shard_map/reduce_scatter | solution.py:19
  406.2 25.8 %copy-start.1 = (f32[128,576]{0,1:T(8,128)S(1)}, f32[128,576]{0,1:T(8,128)}, u32[]{:S(2)}) copy-start(f32[128,576]{0,1:T(8,128)} %reduce-scatter.2.cloned.1.call-done) | copy-start | bytes 884740
  406.2 25.8 %all-to-all-start = ((f32[32,128,64]{1,2,0:T(8,128)}), f32[32,128,64]{1,2,0:T(8,128)S(1)}, u32[]{:S(2)}, u32[]{:S(2)}) async-start(f32[32,128,64]{1,2,0:T(8,128)} %stack.4), calls=%async_computation.1 | async-start | bytes 2097152 | tf_op jit(solution)/shard_map/all_to_all | solution.py:39
  694.9 23.3 %all-to-all-start.1 = ((f32[32,128,64]{1,2,0:T(8,128)}), f32[32,128,64]{1,2,0:T(8,128)S(1)}, u32[]{:S(2)}, u32[]{:S(2)}) async-start(f32[32,128,64]{1,2,0:T(8,128)} %stack.5), calls=%async_computation.2 | async-start | bytes 2097152 | tf_op jit(solution)/shard_map/all_to_all | solution.py:39
Sparse Core Ops, SparseCore 0:
  17.8 92.8 all-gather.1
  120.7 283.5 reduce-scatter.1
